TPU v7x, 32 devices: a whole 2x2x4 slice. The times are simulated.
32 devices in a mesh: grp: 4 (over x, core), pen: 8 (over z, y).
Axes of the slice: x: 2, y: 2, z: 4, core: 2. Of those that a mesh axis runs over, the one named last changes fastest.
Arguments:
- u_field: float32 [2, 2048, 2048], P(None, ('grp', 'pen')), may hold values from -6 to 6
- v_field: float32 [2, 2048, 2048], P(None, ('grp', 'pen')), may hold values from -6 to 6
- ky_order: int32 [2048], replicated, may hold values from 0 to 2047, as said below
Outputs:
- deriv: float32 [2048, 2, 2, 2048], P('grp', None, None, 'pen')
Inputs may be any that keep to these rules, and one draw needn't show every extreme that they name: ky_order is a permutation of 0 to 2047; for every position j, ky_order[2047 - j] = (2048 - ky_order[j]) mod 2048, except for the one pair of positions that holds 0 and 1024.
All inputs are finite; a program needn't handle non-finite values.
Results may differ from a plain program's by a relative error of at most 0.00007.
Values sent between devices are 32-bit elements; how exact they have to be, the bound alone decides.
No kernel may reach another device: no remote copies, remote signals or barrier semaphores. Data moves between devices by JAX's collectives and lax.ppermute only.
A program may use at most 64 MiB of HBM per device.

v0:
```python
import functools
import math

import jax
import jax.numpy as jnp
import numpy as np
from jax import lax
from jax.experimental import pallas as pl
from jax.experimental.pallas import tpu as pltpu
from jax.sharding import PartitionSpec as P


LAST = ((4, 0), (6, 1))
PARTS = {6: 2}
f32 = jnp.float32
bf16 = jnp.bfloat16


def split_two(x):
    high = x.astype(bf16)
    return high, (x - high.astype(f32)).astype(bf16)


def split_three(x):
    high = x.astype(bf16)
    rest = x - high.astype(f32)
    middle = rest.astype(bf16)
    return high, middle, (rest - middle.astype(f32)).astype(bf16)


def dot(a, b):
    return jnp.dot(a, b, preferred_element_type=f32)


def signed_scale(waves, length):
    signed = jnp.where(waves < length // 2, waves, waves - length)
    signed = jnp.where(waves == length // 2, 0, signed)
    return 2.0 / length * signed.astype(f32)


def cos_sin(residue, length):
    eighth = length // 8
    turned = (residue + eighth) & (length - 1)
    turn = turned // (2 * eighth)
    x = (2.0 * math.pi / length) * (turned - turn * (2 * eighth) - eighth).astype(f32)
    y = x * x
    cosine = 1.0 + y * (-1 / 2 + y * (1 / 24 + y * (-1 / 720 + y * (1 / 40320))))
    sine = x * (1.0 + y * (-1 / 6 + y * (1 / 120 + y * (-1 / 5040 + y * (1 / 362880)))))
    odd = (turn & 1) == 1
    first, second = jnp.where(odd, sine, cosine), jnp.where(odd, cosine, sine)
    return (
        jnp.where((turn == 1) | (turn == 2), -first, first),
        jnp.where(turn >= 2, -second, second),
    )


def reverse_lanes(x, swap):
    high, middle, low = split_three(x)
    return dot(high, swap) + (dot(middle, swap) + dot(low, swap))


def transform_block(fields, table_ref, waves, first, slab):
    field_high, field_low = fields
    rows = field_high.shape[0] // 4
    half = table_ref.shape[2] // 2
    sums = []
    for part in range(2):
        columns = pl.ds(part * half + first, slab)
        high, low = table_ref[0, :, columns], table_ref[1, :, columns]
        sums.append(dot(field_high, high) + (dot(field_high, low) + dot(field_low, high)))
    residue = waves & 3
    sign = jnp.where((residue & 1) == 1, -1.0, 1.0)
    cosine = jnp.where(residue == 0, 1.0, jnp.where(residue == 2, -1.0, 0.0))
    sine = jnp.where(residue == 1, 1.0, jnp.where(residue == 3, -1.0, 0.0))

    def folded(x):
        return (
            x[:rows] + sign * x[2 * rows : 3 * rows],
            x[rows : 2 * rows] + sign * x[3 * rows :],
        )

    even_c, odd_c = folded(sums[0])
    even_s, odd_s = folded(sums[1])
    return (
        even_c + cosine * odd_c - sine * odd_s,
        even_s + cosine * odd_s + sine * odd_c,
    )


def cut_pieces(slots):
    return [(k, part, PARTS.get(k, 1)) for k in slots for part in range(PARTS.get(k, 1))]


def fill_table(waves, table_ref, length):
    half = waves.shape[1]
    norm = 1.0 / math.sqrt(length)
    fine = 32
    coarse = length // 4 // fine
    special = (waves == 0) | (waves == length // 2)
    coarse_c, coarse_s = cos_sin(
        (fine * lax.broadcasted_iota(jnp.int32, (coarse, half), 0) * waves) & (length - 1), length
    )
    coarse_c, coarse_s = norm * coarse_c, norm * coarse_s
    index = lax.broadcasted_iota(jnp.int32, (fine, half), 0)
    fine_c, fine_s = cos_sin((index * waves) & (length - 1), length)
    other = norm * jnp.where((waves == 0) & ((index & 1) == 1), -1.0, 1.0)
    for a in range(coarse):
        this_c, this_s = coarse_c[a : a + 1], coarse_s[a : a + 1]
        here = slice(a * fine, (a + 1) * fine)
        cosines = this_c * fine_c - this_s * fine_s
        sines = this_c * fine_s + this_s * fine_c
        sines = jnp.where(special, other, sines)
        for part, values in enumerate((cosines, sines)):
            high, low = split_two(values)
            table_ref[0, here, part * half : (part + 1) * half] = high
            table_ref[1, here, part * half : (part + 1) * half] = low


def load_quarters(ref):
    quarter = ref.shape[1] // 4
    x = jnp.concatenate([ref[:, i * quarter : (i + 1) * quarter] for i in range(4)], 0)
    return split_two(x)


def second_kernel(
    sizes, tile, order_hbm, field_hbm, out_hbm, order_ref, field_ref, table_ref, piece_ref, sems
):
    planes, rows, slab, pens = sizes
    lanes = 128
    first_load = pltpu.make_async_copy(order_hbm, order_ref, sems.at[pens + 1])
    first_load.start()
    load = pltpu.make_async_copy(field_hbm, field_ref, sems.at[pens])
    load.start()
    first_load.wait()
    starts = [block * slab + tile * lanes for block in range(pens // 2)]
    waves = jnp.concatenate([order_ref[:, at : at + lanes] for at in starts], 1)
    fill_table(waves, table_ref, order_ref.shape[1])
    load.wait()
    fields = load_quarters(field_ref)
    copies = []
    for pair in range(pens // 4):
        first = 2 * pair * lanes
        here = waves[:, first : first + 2 * lanes]
        c, s = transform_block(fields, table_ref, here, first, 2 * lanes)
        for side in range(2):
            block = 2 * pair + side
            columns = slice(side * lanes, (side + 1) * lanes)
            for part, values in enumerate((s, c)):
                for plane in range(planes):
                    piece_ref[block, part * planes + plane] = values[
                        plane * rows : (plane + 1) * rows, columns
                    ]
            for target in (block, pens - 1 - block):
                copy = pltpu.make_async_copy(
                    piece_ref.at[block], out_hbm.at[target], sems.at[target]
                )
                copy.start()
                copies.append(copy)
    for copy in copies:
        copy.wait()


def first_kernel(sizes, slots, order_ref, swap_ref, field_hbm, *refs):
    planes, rows, slab, pens = sizes
    outs, (field_ref, table_ref, waves_ref, piece_ref, sems) = refs[:-5], refs[-5:]
    pieces = cut_pieces(range(pens))
    load = pltpu.make_async_copy(field_hbm, field_ref, sems.at[len(outs)])
    load.start()
    length = order_ref.shape[1]
    pen = lax.axis_index("pen")
    upper = pen >= pens // 2
    for i, slot in enumerate(slots):
        target = pen ^ slot
        block = jnp.where(upper, pens - 1 - target, target)
        first = pl.multiple_of(block * slab, slab)
        waves_ref[:, i * slab : (i + 1) * slab] = order_ref[:, pl.ds(first, slab)]
    fill_table(waves_ref[...], table_ref, length)
    load.wait()
    fields = load_quarters(field_ref)
    lanes = 128
    step = 2 * planes * (slab // lanes)
    copies = []
    for i in range(len(slots)):
        waves = waves_ref[:, i * slab : (i + 1) * slab]
        c, s = transform_block(fields, table_ref, waves, i * slab, slab)
        scale = signed_scale(waves, length)
        for part, values in enumerate((scale * s, scale * c)):
            turned = reverse_lanes(values, swap_ref[...])
            if part == 1:
                turned = -turned
            near, far = jnp.where(upper, turned, values), jnp.where(upper, values, turned)
            for to, piece in ((2 * i, near), (2 * i + 1, far)):
                for plane in range(planes):
                    for tile in range(slab // lanes):
                        at = (part * (slab // lanes) + tile) * planes + plane
                        piece_ref[to, pl.ds(at, rows, stride=step), :] = piece[
                            plane * rows : (plane + 1) * rows, tile * lanes : (tile + 1) * lanes
                        ]
        for to, slot in ((2 * i, slots[i]), (2 * i + 1, pens - 1 - slots[i])):
            for n, (other, part, parts) in enumerate(pieces):
                if other != slot:
                    continue
                height = rows * step // parts
                copy = pltpu.make_async_copy(
                    piece_ref.at[to, part * height : (part + 1) * height], outs[n], sems.at[n]
                )
                copy.start()
                copies.append(copy)
    for copy in copies:
        copy.wait()


def table_kernel(after_ref, out_ref):
    width = out_ref.shape[2]
    length = 8 * width
    rows = 64
    for distance in range(4):
        for at in range(0, width, rows):
            n = (
                lax.broadcasted_iota(jnp.int32, (rows, width), 0)
                - lax.broadcasted_iota(jnp.int32, (rows, width), 1)
                + (distance * width + at)
            )
            cosine, sine = cos_sin(n & (length - 1), length)
            factor = jnp.where((n & 1) == 1, 1.0 / length, -1.0 / length)
            inverse = jnp.where(n == 0, 0.0, factor / jnp.where(n == 0, 1.0, sine))
            here = slice(at, at + rows)
            for i, part in enumerate(split_two(cosine * inverse)):
                out_ref[i, distance, here, :] = part
            for i, part in enumerate(split_two(inverse)):
                out_ref[i, 4 + distance, here, :] = part
                if distance:
                    out_ref[i, 7 + distance, here, :] = -part


def circulant_kernel(recv_ref, table_ref, turn_ref, *out_refs):
    count, rows, lanes = recv_ref.shape
    width = count * rows // 8
    turn = turn_ref[...]
    top, bottom = [
        jnp.concatenate(
            [recv_ref[4 * pen + group] for group in groups for pen in range(count // 4)], 0
        )
        for groups in ((0, 1), (2, 3))
    ]

    def operand(x):
        return dot(jnp.concatenate(split_two(x), 1), turn).astype(bf16)

    plus, minus = operand(top + bottom), operand(top - bottom)
    for pair in range(2):
        group = lax.axis_index("grp") ^ pair
        swapped = group >= 2
        for i in range(2):
            row = 2 * (group & 1) + i

            def product(x, index):
                both = jnp.concatenate(
                    [
                        jnp.concatenate([table_ref[w, index(column)] for column in range(4)], 1)
                        for w in range(2)
                    ],
                    0,
                )
                both = dot(both, x)
                return both[:width, :lanes] + (both[:width, lanes:] + both[width:, :lanes])

            even = product(plus, lambda column: (row - column) & 3)
            odd = product(
                minus, lambda column: row - column + jnp.where(row >= column, 4, 11)
            )
            here = slice(i * width, (i + 1) * width)
            out_refs[pair][here, :] = even + jnp.where(swapped, -odd, odd)
            out_refs[pair + 2][here, :] = even + jnp.where(swapped, odd, -odd)


def final_kernel(sizes, early, late, order_ref, *refs):
    planes, rows, slab, pens = sizes
    lanes = 128
    tiles = slab // lanes
    step = 2 * planes * tiles
    count = 4 * tiles
    firsts, seconds = refs[: len(early)], refs[len(early) : len(early) + count]
    out_hbm, late_refs, (piece_ref, sems) = refs[-3 - len(late)], refs[-2 - len(late) : -2], refs[-2:]
    pen, group = lax.axis_index("pen"), lax.axis_index("grp")
    upper = pen >= pens // 2
    low_bit, high_bit = (group & 1) == 1, group >= 2
    waves = order_ref[:, pl.ds(pl.multiple_of(pen * slab, slab), slab)]
    specials = (waves == 0) | (waves == order_ref.shape[1] // 2)
    stores = []
    for at, (slot, part_at, parts) in enumerate([*early, *late]):
        source = pen ^ slot
        height = rows // parts
        first = pl.multiple_of(source * rows + part_at * height, height)
        is_early = at < len(early)
        r = [ref[pl.ds(first, height), :] for ref in seconds]
        r = [jnp.where(low_bit, r[k ^ 1], r[k]) for k in range(count)]
        r = [jnp.where(high_bit, r[k ^ 2], r[k]) for k in range(count)]
        if tiles == 2:
            r = [jnp.where(upper, r[k ^ 4], r[k]) for k in range(count)]
        for tile in range(tiles):
            special = specials[:, tile * lanes : (tile + 1) * lanes]
            base = 4 * tile
            for plane in range(planes):
                s, c = r[base + plane], r[base + planes + plane]
                pieces = (
                    jnp.where(special, 0.0, jnp.where(upper, s, -s)),
                    jnp.where(special & upper, -s, -c),
                )
                for part in range(2):
                    there = pl.ds((part * tiles + tile) * planes + plane, height, stride=step)
                    if is_early:
                        piece_ref[at, there, :] = firsts[at][there, :] + pieces[part]
                    else:
                        late_refs[at - len(early)][there, :] = pieces[part]
        if is_early:
            store = pltpu.make_async_copy(
                piece_ref.at[at, : height * step],
                out_hbm.at[pl.ds(first * step, height * step)],
                sems.at[at],
            )
            store.start()
            stores.append(store)
    for store in stores:
        store.wait()


def last_kernel(pieces, *refs):
    count = len(pieces)
    lates, firsts, (before_hbm, out_hbm, piece_ref, sems) = (
        refs[:count],
        refs[count : 2 * count],
        refs[2 * count :],
    )
    stores = []
    for at, (slot, part, parts) in enumerate(pieces):
        size = lates[at].shape[0]
        first = ((lax.axis_index("pen") ^ slot) * parts + part) * size
        piece_ref[at, :size] = firsts[at][...] + lates[at][...]
        store = pltpu.make_async_copy(
            piece_ref.at[at, :size],
            out_hbm.at[pl.ds(pl.multiple_of(first, size), size)],
            sems.at[at],
        )
        store.start()
        stores.append(store)
    for store in stores:
        store.wait()


SPACES = {"s": pltpu.SMEM, "v": pltpu.VMEM, "h": pltpu.HBM, "a": pl.ANY}


def kernel_call(body, shapes, spaces, flops, moved, limit, scratch=(), aliases=None):
    inputs, outputs = spaces.split(">")
    specs = [pl.BlockSpec(memory_space=SPACES[s]) for s in outputs]
    return pl.pallas_call(
        body,
        out_shape=shapes,
        in_specs=[pl.BlockSpec(memory_space=SPACES[s]) for s in inputs],
        out_specs=specs if isinstance(shapes, list) else specs[0],
        scratch_shapes=scratch,
        input_output_aliases=aliases or {},
        cost_estimate=pl.CostEstimate(flops=flops, bytes_accessed=moved, transcendentals=0),
        compiler_params=pltpu.CompilerParams(vmem_limit_bytes=limit * 2**20),
    )


def exchange(block, axis, distance):
    size = lax.axis_size(axis)
    return lax.ppermute(block, axis, [(i, i ^ distance) for i in range(size)])


def fast_path(u, v, ky_order, sizes, groups):
    planes, rows, slab, pens = sizes
    length_y = v.shape[1]
    group_rows = rows * pens
    length_z = group_rows * groups
    half = length_y // 2
    lanes = 128
    pen = lax.axis_index("pen")
    order = ky_order[None, :]
    flops = 2 * 3 * planes * rows * length_y * length_y
    dma = pltpu.SemaphoreType.DMA
    field = pltpu.VMEM(v.shape, f32)
    tiles = slab // lanes
    recv = []
    for tile in range(tiles):
        v_blocks = kernel_call(
            functools.partial(second_kernel, sizes, tile),
            jax.ShapeDtypeStruct((pens, 2 * planes, rows, lanes), f32),
            "hh>h",
            flops // tiles,
            2**21,
            60,
            [
                pltpu.VMEM((1, length_y), jnp.int32),
                field,
                pltpu.VMEM((2, length_y // 4, length_y // tiles), bf16),
                pltpu.VMEM((pens // 2, 2 * planes, rows, lanes), f32),
                dma((pens + 2,)),
            ],
        )(order, v)
        v_blocks = v_blocks.reshape(groups * pens, rows, lanes)
        recv.append(lax.all_to_all(v_blocks, ("pen", "grp"), 0, 0, tiled=True))
    swap = jnp.asarray(np.eye(slab)[::-1].copy(), bf16)
    size = rows * 2 * planes * slab // lanes
    pieces = cut_pieces(range(pens))
    half_pens = list(range(pens // 2))
    firsts = kernel_call(
        functools.partial(first_kernel, sizes, half_pens),
        [jax.ShapeDtypeStruct((size // parts, lanes), f32) for _, _, parts in pieces],
        "vvh>" + "h" * len(pieces),
        flops,
        2**21,
        60,
        [
            field,
            pltpu.VMEM((2, length_y // 4, length_y), bf16),
            pltpu.VMEM((1, half), jnp.int32),
            pltpu.VMEM((pens, size, lanes), f32),
            dma((len(pieces) + 1,)),
        ],
    )(order, swap, u)
    firsts = dict(zip(pieces, firsts))
    circulant = kernel_call(
        table_kernel,
        jax.ShapeDtypeStruct((2, 11, length_z // 8, length_z // 8), bf16),
        "a>v",
        2**24,
        2**21,
        16,
    )(firsts[pieces[0]])
    arrived = {}
    for piece in pieces:
        k, _, _ = piece
        arrived[piece] = exchange(firsts[piece], "pen", k) if k else firsts[piece]
    flip = np.kron(np.eye(2), np.eye(lanes)[::-1])
    turn = jnp.where(pen >= pens // 2, jnp.asarray(flip, bf16), jnp.asarray(np.eye(2 * lanes), bf16))
    seconds = []
    for tile in range(tiles):
        parts = kernel_call(
            circulant_kernel,
            [jax.ShapeDtypeStruct((group_rows, lanes), f32)] * groups,
            "vvv>vvvv",
            3 * length_z * length_z * lanes,
            2**22,
            20,
        )(recv[tile], circulant, turn)
        seconds.append(parts[0])
        for k in range(1, groups):
            seconds.append(exchange(parts[k], "grp", k))
    early = [piece for piece in pieces if piece[:2] not in LAST]
    late = [piece for piece in pieces if piece[:2] in LAST]
    late_shapes = [jax.ShapeDtypeStruct((size // parts, lanes), f32) for _, _, parts in late]
    result, *rest = kernel_call(
        functools.partial(final_kernel, sizes, early, late),
        [jax.ShapeDtypeStruct((pens * size, lanes), f32), *late_shapes],
        "v" + "v" * (len(early) + groups * tiles) + ">h" + "v" * len(late),
        2**20,
        2**20,
        16,
        [pltpu.VMEM((len(early), size, lanes), f32), dma((len(early),))],
    )(order, *[arrived[piece] for piece in early], *seconds)
    tall = max(shape.shape[0] for shape in late_shapes)
    result = kernel_call(
        functools.partial(last_kernel, late),
        jax.ShapeDtypeStruct(result.shape, f32),
        "v" * (2 * len(late)) + "h>h",
        2**18,
        2**18,
        8,
        [pltpu.VMEM((len(late), tall, lanes), f32), dma((len(late),))],
        {2 * len(late): 0},
    )(*rest, *[arrived[piece] for piece in late], result)
    result = result.reshape(group_rows, 2, tiles, planes, lanes)
    return jnp.transpose(result, (0, 1, 3, 2, 4)).reshape(group_rows, 2, planes, slab)


def whole_tables(length):
    half = length // 2
    n = lax.broadcasted_iota(jnp.int32, (half, half), 0) - lax.broadcasted_iota(
        jnp.int32, (half, half), 1
    )
    theta = 2.0 * math.pi / length * n.astype(f32)
    factor = jnp.where(n % 2 == 0, -1.0 / length, 1.0 / length)
    inverse = jnp.where(n == 0, 0.0, factor / jnp.where(n == 0, 1.0, jnp.sin(theta)))
    return jnp.cos(theta) * inverse, inverse


def plain_path(u, v, ky_order, sizes, groups):
    planes, rows, slab, pens = sizes
    length_y = v.shape[1]
    group_rows = rows * pens
    length_z = group_rows * groups
    half = length_y // 2
    exact = lax.Precision.HIGHEST
    pen = lax.axis_index("pen")
    upper = pen >= pens // 2
    waves = ky_order[:half]
    index = lax.iota(jnp.int32, length_y)[:, None]
    theta = 2.0 * math.pi / length_y * (index * waves[None, :] % length_y).astype(f32)
    mixed = 2.0 * math.pi / length_y * (index * (half - waves[None, :]) % length_y).astype(f32)
    special = (waves == 0) | (waves == half)
    sines = jnp.where(special, jnp.cos(mixed), jnp.sin(theta))
    both = 1.0 / math.sqrt(length_y) * jnp.stack([sines, jnp.cos(theta)])

    def transform(x):
        y = jnp.einsum("ry,pyk->prk", x, both, precision=exact)
        return y.reshape(2, planes, rows, pens // 2, slab)

    y = transform(v)
    y = jnp.concatenate([y, jnp.flip(y, 3)], 3)
    v_blocks = jnp.transpose(y, (3, 2, 0, 1, 4)).reshape(pens, rows, groups, -1)
    v_blocks = jnp.transpose(v_blocks, (2, 0, 1, 3)).reshape(groups * pens, rows, -1)
    y = transform(u) * signed_scale(waves, length_y).reshape(pens // 2, slab)
    turned = jnp.flip(y, (3, 4)) * jnp.array([1.0, -1.0], f32)[:, None, None, None, None]
    u_blocks = jnp.transpose(jnp.concatenate([y, turned], 3), (3, 2, 0, 1, 4))
    recv = lax.all_to_all(v_blocks, ("grp", "pen"), 0, 0, tiled=True).reshape(length_z, -1)
    u_recv = lax.all_to_all(u_blocks, "pen", 0, 0, tiled=True)
    table = whole_tables(length_z)
    top, bottom = recv[: length_z // 2], recv[length_z // 2 :]
    even = jnp.dot(table[0], top + bottom, precision=exact)
    odd = jnp.dot(table[1], top - bottom, precision=exact)
    deriv = jnp.concatenate([even + odd, even - odd], 0)
    back = lax.all_to_all(deriv.reshape(groups, group_rows, -1), "grp", 0, 0, tiled=True)
    back = jnp.transpose(back, (1, 0, 2)).reshape(group_rows, 2, planes, slab)
    back = jnp.where(upper, jnp.flip(back, 3), back)
    mine = lax.dynamic_slice_in_dim(ky_order, pen * slab, slab)
    special = (mine == 0) | (mine == half)
    s, c = back[:, 0], back[:, 1]
    first = jnp.where(special, 0.0, jnp.where(upper, s, -s))
    second = jnp.where(special & upper, -s, -c)
    return u_recv.reshape(group_rows, 2, planes, slab) + jnp.stack([first, second], 1)


def on_device(u_field, v_field, ky_order):
    planes, rows, length_y = u_field.shape
    pens, groups = lax.axis_size("pen"), lax.axis_size("grp")
    slab = length_y // pens
    u = u_field.reshape(planes * rows, length_y)
    v = v_field.reshape(planes * rows, length_y)
    fast = slab % 128 == 0 and rows % 8 == 0 and groups == 4 and planes == 2 and pens % 4 == 0
    fast = fast and length_y % 1024 == 0 and length_y & (length_y - 1) == 0 and pens & (pens - 1) == 0
    path = fast_path if fast else plain_path
    return path(u, v, ky_order, (planes, rows, slab, pens), groups)


def solution(mesh):
    placed = (P(None, ("grp", "pen"), None), P(None, ("grp", "pen"), None), P())

    return jax.shard_map(
        on_device,
        mesh=mesh,
        in_specs=placed,
        out_specs=P("grp", None, None, "pen"),
        check_vma=False,
    )
```

profile of v0, /device:TPU:0, one launch (start us, length us, event | category | flops | bytes accessed | tf_op | source)
XLA Modules:
  0.0 115.3 jit_solution(10560022583144614825)
XLA Ops:
  0.0 4.1 %shard_map.68 = f32[8,4,64,128]{3,2,1,0:T(8,128)} custom-call(s32[1,2048]{1,0:T(1,128)} %bitcast.10, f32[128,2048]{1,0:T(8,128)} %bitcast.16), custom_call_target="tpu_custom_call" | custom-call | flops 1610612736 | bytes 2097152 | tf_op jit(solution)/shard_map/pallas_call | solution.py:389
  4.1 7.3 %all-to-all-start.1 = ((f32[32,64,128]{2,1,0:T(8,128)}), f32[32,64,128]{2,1,0:T(8,128)S(1)}, u32[]{:S(2)}, u32[]{:S(2)}) async-start(f32[32,64,128]{2,1,0:T(8,128)} %bitcast.15), calls=%async_computation.1 | async-start | bytes 2097152 | tf_op jit(solution)/shard_map/all_to_all | solution.py:405
  11.5 4.1 %shard_map.65 = f32[8,4,64,128]{3,2,1,0:T(8,128)} custom-call(s32[1,2048]{1,0:T(1,128)} %bitcast.11, f32[128,2048]{1,0:T(8,128)} %bitcast.17), custom_call_target="tpu_custom_call" | custom-call | flops 1610612736 | bytes 2097152 | tf_op jit(solution)/shard_map/pallas_call | solution.py:389
  15.6 22.1 %all-to-all-done.1.recv_ref = f32[32,64,128]{2,1,0:T(8,128)S(1)} async-done(((f32[32,64,128]{2,1,0:T(8,128)}), f32[32,64,128]{2,1,0:T(8,128)S(1)}, u32[]{:S(2)}, u32[]{:S(2)}) %all-to-all-start.1) | async-done | bytes 1048608 | tf_op jit(solution)/shard_map/all_to_all | solution.py:405
  37.7 0.0 copy-start
  37.7 3.9 %all-to-all-start = ((f32[32,64,128]{2,1,0:T(8,128)}), f32[32,64,128]{2,1,0:T(8,128)}, u32[]{:S(2)}, u32[]{:S(2)}) async-start(f32[32,64,128]{2,1,0:T(8,128)} %bitcast.14), calls=%async_computation | async-start | bytes 2097152 | tf_op jit(solution)/shard_map/all_to_all | solution.py:405
  41.6 0.0 copy-start.9
  41.6 0.0 copy-start.10
  41.6 8.3 %shard_map.64 = (f32[512,128]{1,0:T(8,128)}, f32[512,128]{1,0:T(8,128)}, f32[512,128]{1,0:T(8,128)}, f32[512,128]{1,0:T(8,128)}, f32[512,128]{1,0:T(8,128)}, /*i...) custom-call(s32[1,2048]{1,0:T(1,128)} %bitcast.12, ...), custom_call_target="tpu_custom_call" | custom-call | flops 3221225472 | bytes 2097152 | tf_op jit(solution)/shard_map/pallas_call | solution.py:410
  49.9 0.0 copy-done
  49.9 3.6 %collective-permute-start.4 = (f32[256,128]{1,0:T(8,128)}, f32[256,128]{1,0:T(8,128)}, u32[]{:S(2)}, u32[]{:S(2)}) collective-permute-start(f32[256,128]{1,0:T(8,128)} %get-tuple-element.30), channel_id=1, source_target_pairs={{0,6},{1,7},{2,4},{3,5},{4,2},{5,3},{6,0},{7,1},{8,14},{9,15},{10,... | collective-permute-start | bytes 393224 | tf_op jit(solution)/shard_map/ppermute | solution.py:371
  53.6 1.5 %collective-permute-start = (f32[512,128]{1,0:T(8,128)}, f32[512,128]{1,0:T(8,128)S(1)}, u32[]{:S(2)}, u32[]{:S(2)}) collective-permute-start(f32[512,128]{1,0:T(8,128)} %get-tuple-element.26), channel_id=1, source_target_pairs={{0,1},{1,0},{2,3},{3,2},{4,5},{5,4},{6,7},{7,6},{8,9},{9,8},{10,11... | collective-permute-start | bytes 786440 | tf_op jit(solution)/shard_map/ppermute | solution.py:371
  55.0 0.0 collective-permute-start.1
  55.0 2.0 %collective-permute-start.2 = (f32[512,128]{1,0:T(8,128)}, f32[512,128]{1,0:T(8,128)}, u32[]{:S(2)}, u32[]{:S(2)}) collective-permute-start(f32[512,128]{1,0:T(8,128)} %get-tuple-element.28), channel_id=1, source_target_pairs={{0,3},{1,2},{2,1},{3,0},{4,7},{5,6},{6,5},{7,4},{8,11},{9,10},{10,... | collective-permute-start | bytes 786440 | tf_op jit(solution)/shard_map/ppermute | solution.py:371
  57.0 0.5 collective-permute-start.3
  57.6 0.0 copy-done.9
  57.6 0.0 copy-done.10
  57.6 0.0 copy-start.1
  57.6 0.0 copy-start.2
  57.6 1.0 copy-done.2
  58.6 2.5 %shard_map.66.table_ref = bf16[2,11,256,256]{3,2,1,0:T(8,128)(2,1)S(1)} custom-call(f32[512,128]{1,0:T(8,128)S(1)} %copy-done.2), custom_call_target="tpu_custom_call" | custom-call | flops 16777216 | bytes 2097152 | tf_op jit(solution)/shard_map/pallas_call | solution.py:426
  61.1 0.0 copy-done.1
  61.1 3.5 %shard_map.69 = (f32[512,128]{1,0:T(8,128)S(1)}, f32[512,128]{1,0:T(8,128)}, f32[512,128]{1,0:T(8,128)}, f32[512,128]{1,0:T(8,128)}) custom-call(f32[32,64,128]{2,1,0:T(8,128)S(1)} %copy-done.1, bf16[2,11,256,256]{3,2,1,0:T(8,128)(2,1)S(1)} %shard_map.66.table_ref, bf16[256,256]{1,0:T(8,128)(2,1)S(1)} %broadcast_select_fusion.turn_ref), custom_call_target="tpu_custom_call" | custom-call | flops 1610612736 | bytes 4194304 | tf_op jit(solution)/shard_map/pallas_call | solution.py:442
  64.6 0.0 copy-start.6
  64.6 0.7 copy-done.6
  65.3 1.0 collective-permute-done.4.refs_5_
  66.3 1.8 %collective-permute-start.5 = (f32[512,128]{1,0:T(8,128)}, f32[512,128]{1,0:T(8,128)}, u32[]{:S(2)}, u32[]{:S(2)}) collective-permute-start(f32[512,128]{1,0:T(8,128)} %get-tuple-element.31), channel_id=1, source_target_pairs={{0,7},{1,6},{2,5},{3,4},{4,3},{5,2},{6,1},{7,0},{8,15},{9,14},{10,... | collective-permute-start | bytes 786440 | tf_op jit(solution)/shard_map/ppermute | solution.py:371
  68.1 0.0 collective-permute-done.refs_1_
  68.1 0.0 collective-permute-start.9
  68.1 3.8 %collective-permute-done.1.refs_2_ = f32[512,128]{1,0:T(8,128)S(1)} collective-permute-done((f32[512,128]{1,0:T(8,128)}, f32[512,128]{1,0:T(8,128)S(1)}, u32[]{:S(2)}, u32[]{:S(2)}) %collective-permute-start.1) | collective-permute-done | bytes 262176 | tf_op jit(solution)/shard_map/ppermute | solution.py:371
  71.9 0.0 copy-start.4
  71.9 0.7 copy-done.4
  72.6 1.0 collective-permute-start.10
  73.6 7.1 %collective-permute-done.2.refs_3_ = f32[512,128]{1,0:T(8,128)} collective-permute-done((f32[512,128]{1,0:T(8,128)}, f32[512,128]{1,0:T(8,128)}, u32[]{:S(2)}, u32[]{:S(2)}) %collective-permute-start.2) | collective-permute-done | bytes 262176 | tf_op jit(solution)/shard_map/ppermute | solution.py:371
  80.7 0.0 copy-start.3
  80.7 0.0 copy-start.8
  80.7 0.8 collective-permute-start.11
  81.4 0.0 all-to-all-done.recv_ref
  81.4 0.0 copy-start.12
  81.5 0.0 copy-start.7
  81.5 4.0 %shard_map.67 = (f32[512,128]{1,0:T(8,128)S(1)}, f32[512,128]{1,0:T(8,128)S(1)}, f32[512,128]{1,0:T(8,128)S(1)}, f32[512,128]{1,0:T(8,128)S(1)}) custom-call(f32[32,64,128]{2,1,0:T(8,128)} %all-to-all-done.recv_ref, bf16[2,11,256,256]{3,2,1,0:T(8,128)(2,1)S(1)} %shard_map.66.table_ref, bf16[256,256]{1,0:T(8,128)(2,1)S(1)} %broadcast_select_fusion.turn_ref), custom_call_target="tpu_custom_call" | custom-call | flops 1610612736 | bytes 4194304 | tf_op jit(solution)/shard_map/pallas_call | solution.py:442
  85.5 6.1 %collective-permute-done.3.refs_4_ = f32[512,128]{1,0:T(8,128)} collective-permute-done((f32[512,128]{1,0:T(8,128)}, f32[512,128]{1,0:T(8,128)}, u32[]{:S(2)}, u32[]{:S(2)}) %collective-permute-start.3) | collective-permute-done | bytes 262176 | tf_op jit(solution)/shard_map/ppermute | solution.py:371
  91.6 0.0 collective-permute-start.6
  91.6 0.0 collective-permute-done.5.refs_6_
  91.6 1.5 %collective-permute-start.7 = (f32[512,128]{1,0:T(8,128)S(1)}, f32[512,128]{1,0:T(8,128)S(1)}, u32[]{:S(2)}, u32[]{:S(2)}) collective-permute-start(f32[512,128]{1,0:T(8,128)S(1)} %get-tuple-element.34), channel_id=1, source_target_pairs={{0,16},{8,24},{16,0},{24,8},{1,17},{9,25},{17,1},{25,9},{2,18},{10... | collective-permute-start | bytes 786440 | tf_op jit(solution)/shard_map/ppermute | solution.py:371
  93.1 0.0 collective-permute-done.9.refs_12_
  93.1 0.4 collective-permute-start.8
  93.5 0.0 collective-permute-done.10.refs_13_
  93.5 0.0 copy-done.11
  93.5 5.3 %collective-permute-start.12 = (f32[512,128]{1,0:T(8,128)S(1)}, f32[512,128]{1,0:T(8,128)S(1)}, u32[]{:S(2)}, u32[]{:S(2)}) collective-permute-start(f32[512,128]{1,0:T(8,128)S(1)} %copy-done.11), channel_id=1, source_target_pairs={{0,4},{1,5},{2,6},{3,7},{4,0},{5,1},{6,2},{7,3},{8,12},{9,13},{10,... | collective-permute-start | bytes 786440 | tf_op jit(solution)/shard_map/ppermute | solution.py:371
  98.7 0.0 collective-permute-done.11.refs_14_
  98.7 0.0 copy-done.12
  98.7 2.4 %collective-permute-start.13 = (f32[256,128]{1,0:T(8,128)S(1)}, f32[256,128]{1,0:T(8,128)S(1)}, u32[]{:S(2)}, u32[]{:S(2)}) collective-permute-start(f32[256,128]{1,0:T(8,128)S(1)} %copy-done.12), channel_id=1, source_target_pairs={{0,6},{1,7},{2,4},{3,5},{4,2},{5,3},{6,0},{7,1},{8,14},{9,15},{10,... | collective-permute-start | bytes 393224 | tf_op jit(solution)/shard_map/ppermute | solution.py:371
  101.2 0.0 collective-permute-done.6.refs_8_
  101.2 0.0 collective-permute-done.7.refs_9_
  101.2 4.3 %collective-permute-done.8.refs_10_ = f32[512,128]{1,0:T(8,128)S(1)} collective-permute-done((f32[512,128]{1,0:T(8,128)S(1)}, f32[512,128]{1,0:T(8,128)S(1)}, u32[]{:S(2)}, u32[]{:S(2)}) %collective-permute-start.8) | collective-permute-done | bytes 262176 | tf_op jit(solution)/shard_map/ppermute | solution.py:371
  105.5 0.0 copy-done.3
  105.5 0.0 copy-done.8
  105.5 0.0 copy-done.5
  105.5 0.0 copy-done.7
  105.5 2.9 %shard_map.70 = (f32[4096,128]{1,0:T(8,128)}, f32[512,128]{1,0:T(8,128)S(1)}, f32[256,128]{1,0:T(8,128)S(1)}) custom-call(s32[1,2048]{1,0:T(1,128)S(1)} %bitcast.13, f32[512,128]{1,0:T(8,128)S(1)} %copy-done.3, f32[512,128]{1,0:T(8,128)S(1)} %collective-permute-done.refs_1_, f32[512,128]{1,0:T(8,128)S(1)} %copy-done.5, ...), custom_call_target="tpu_custom_call" | custom-call | flops 1048576 | bytes 1048576 | tf_op jit(solution)/shard_map/pallas_call | solution.py:456
  108.4 2.4 %collective-permute-done.13.refs_3_ = f32[256,128]{1,0:T(8,128)S(1)} collective-permute-done((f32[256,128]{1,0:T(8,128)S(1)}, f32[256,128]{1,0:T(8,128)S(1)}, u32[]{:S(2)}, u32[]{:S(2)}) %collective-permute-start.13) | collective-permute-done | bytes 131104 | tf_op jit(solution)/shard_map/ppermute | solution.py:371
  110.8 3.5 %collective-permute-done.12.refs_2_ = f32[512,128]{1,0:T(8,128)S(1)} collective-permute-done((f32[512,128]{1,0:T(8,128)S(1)}, f32[512,128]{1,0:T(8,128)S(1)}, u32[]{:S(2)}, u32[]{:S(2)}) %collective-permute-start.12) | collective-permute-done | bytes 262176 | tf_op jit(solution)/shard_map/ppermute | solution.py:371
  114.3 0.8 shard_map.71
  (3 shorter events, 0.0 us)
Async XLA Ops:
  4.1 33.5 %all-to-all-start.1 = ((f32[32,64,128]{2,1,0:T(8,128)}), f32[32,64,128]{2,1,0:T(8,128)S(1)}, u32[]{:S(2)}, u32[]{:S(2)}) async-start(f32[32,64,128]{2,1,0:T(8,128)} %bitcast.15), calls=%async_computation.1 | async-start | bytes 2097152 | tf_op jit(solution)/shard_map/all_to_all | solution.py:405
  37.7 12.3 %copy-start = (f32[32,64,128]{2,1,0:T(8,128)}, f32[32,64,128]{2,1,0:T(8,128)S(1)}, u32[]{:S(2)}) copy-start(f32[32,64,128]{2,1,0:T(8,128)S(1)} %all-to-all-done.1.recv_ref) | copy-start | bytes 3145732
  37.7 43.8 %all-to-all-start = ((f32[32,64,128]{2,1,0:T(8,128)}), f32[32,64,128]{2,1,0:T(8,128)}, u32[]{:S(2)}, u32[]{:S(2)}) async-start(f32[32,64,128]{2,1,0:T(8,128)} %bitcast.14), calls=%async_computation | async-start | bytes 2097152 | tf_op jit(solution)/shard_map/all_to_all | solution.py:405
  41.6 16.0 %copy-start.9 = (bf16[256,256]{1,0:T(8,128)(2,1)S(1)}, bf16[256,256]{1,0:T(8,128)(2,1)}, u32[]{:S(2)}) copy-start(bf16[256,256]{1,0:T(8,128)(2,1)} %constant.14.clone) | copy-start | bytes 393220
  41.6 15.9 %copy-start.10 = (bf16[256,256]{1,0:T(8,128)(2,1)S(1)}, bf16[256,256]{1,0:T(8,128)(2,1)}, u32[]{:S(2)}) copy-start(bf16[256,256]{1,0:T(8,128)(2,1)} %constant.13.clone) | copy-start | bytes 393220
  49.9 16.4 %collective-permute-start.4 = (f32[256,128]{1,0:T(8,128)}, f32[256,128]{1,0:T(8,128)}, u32[]{:S(2)}, u32[]{:S(2)}) collective-permute-start(f32[256,128]{1,0:T(8,128)} %get-tuple-element.30), channel_id=1, source_target_pairs={{0,6},{1,7},{2,4},{3,5},{4,2},{5,3},{6,0},{7,1},{8,14},{9,15},{10,... | collective-permute-start | bytes 393224 | tf_op jit(solution)/shard_map/ppermute | solution.py:371
  53.6 14.5 %collective-permute-start = (f32[512,128]{1,0:T(8,128)}, f32[512,128]{1,0:T(8,128)S(1)}, u32[]{:S(2)}, u32[]{:S(2)}) collective-permute-start(f32[512,128]{1,0:T(8,128)} %get-tuple-element.26), channel_id=1, source_target_pairs={{0,1},{1,0},{2,3},{3,2},{4,5},{5,4},{6,7},{7,6},{8,9},{9,8},{10,11... | collective-permute-start | bytes 786440 | tf_op jit(solution)/shard_map/ppermute | solution.py:371
  55.0 16.8 %collective-permute-start.1 = (f32[512,128]{1,0:T(8,128)}, f32[512,128]{1,0:T(8,128)S(1)}, u32[]{:S(2)}, u32[]{:S(2)}) collective-permute-start(f32[512,128]{1,0:T(8,128)} %get-tuple-element.27), channel_id=1, source_target_pairs={{0,2},{1,3},{2,0},{3,1},{4,6},{5,7},{6,4},{7,5},{8,10},{9,11},{10,... | collective-permute-start | bytes 786440 | tf_op jit(solution)/shard_map/ppermute | solution.py:371
  55.0 25.6 %collective-permute-start.2 = (f32[512,128]{1,0:T(8,128)}, f32[512,128]{1,0:T(8,128)}, u32[]{:S(2)}, u32[]{:S(2)}) collective-permute-start(f32[512,128]{1,0:T(8,128)} %get-tuple-element.28), channel_id=1, source_target_pairs={{0,3},{1,2},{2,1},{3,0},{4,7},{5,6},{6,5},{7,4},{8,11},{9,10},{10,... | collective-permute-start | bytes 786440 | tf_op jit(solution)/shard_map/ppermute | solution.py:371
  57.0 34.6 %collective-permute-start.3 = (f32[512,128]{1,0:T(8,128)}, f32[512,128]{1,0:T(8,128)}, u32[]{:S(2)}, u32[]{:S(2)}) collective-permute-start(f32[512,128]{1,0:T(8,128)} %get-tuple-element.29), channel_id=1, source_target_pairs={{0,5},{1,4},{2,7},{3,6},{4,1},{5,0},{6,3},{7,2},{8,13},{9,12},{10,... | collective-permute-start | bytes 786440 | tf_op jit(solution)/shard_map/ppermute | solution.py:371
  57.6 3.5 %copy-start.1 = (f32[32,64,128]{2,1,0:T(8,128)S(1)}, f32[32,64,128]{2,1,0:T(8,128)}, u32[]{:S(2)}) copy-start(f32[32,64,128]{2,1,0:T(8,128)} %copy-done) | copy-start | bytes 3145732
  57.6 1.0 copy-start.2
  64.6 0.7 copy-start.6
  66.3 25.3 %collective-permute-start.5 = (f32[512,128]{1,0:T(8,128)}, f32[512,128]{1,0:T(8,128)}, u32[]{:S(2)}, u32[]{:S(2)}) collective-permute-start(f32[512,128]{1,0:T(8,128)} %get-tuple-element.31), channel_id=1, source_target_pairs={{0,7},{1,6},{2,5},{3,4},{4,3},{5,2},{6,1},{7,0},{8,15},{9,14},{10,... | collective-permute-start | bytes 786440 | tf_op jit(solution)/shard_map/ppermute | solution.py:371
  68.1 25.0 %collective-permute-start.9 = (f32[512,128]{1,0:T(8,128)}, f32[512,128]{1,0:T(8,128)}, u32[]{:S(2)}, u32[]{:S(2)}) collective-permute-start(f32[512,128]{1,0:T(8,128)} %get-tuple-element.37), channel_id=1, source_target_pairs={{0,8},{8,0},{16,24},{24,16},{1,9},{9,1},{17,25},{25,17},{2,10},{10... | collective-permute-start | bytes 786440 | tf_op jit(solution)/shard_map/ppermute | solution.py:371
  71.9 0.7 copy-start.4
  72.6 20.8 %collective-permute-start.10 = (f32[512,128]{1,0:T(8,128)}, f32[512,128]{1,0:T(8,128)}, u32[]{:S(2)}, u32[]{:S(2)}) collective-permute-start(f32[512,128]{1,0:T(8,128)} %get-tuple-element.38), channel_id=1, source_target_pairs={{0,16},{8,24},{16,0},{24,8},{1,17},{9,25},{17,1},{25,9},{2,18},{10... | collective-permute-start | bytes 786440 | tf_op jit(solution)/shard_map/ppermute | solution.py:371
  80.7 24.8 %copy-start.3 = (f32[512,128]{1,0:T(8,128)S(1)}, f32[512,128]{1,0:T(8,128)}, u32[]{:S(2)}) copy-start(f32[512,128]{1,0:T(8,128)} %get-tuple-element.25.after_ref.refs_0_) | copy-start | bytes 786436
  80.7 24.8 %copy-start.8 = (s32[2048]{0:T(1024)S(1)}, s32[2048]{0:T(1024)}, u32[]{:S(2)}) copy-start(s32[2048]{0:T(1024)} %param.8) | copy-start | bytes 24580
  80.7 18.1 %collective-permute-start.11 = (f32[512,128]{1,0:T(8,128)}, f32[512,128]{1,0:T(8,128)}, u32[]{:S(2)}, u32[]{:S(2)}) collective-permute-start(f32[512,128]{1,0:T(8,128)} %get-tuple-element.39), channel_id=1, source_target_pairs={{0,24},{8,16},{16,8},{24,0},{1,25},{9,17},{17,9},{25,1},{2,26},{10... | collective-permute-start | bytes 786440 | tf_op jit(solution)/shard_map/ppermute | solution.py:371
  81.4 12.0 %copy-start.11 = (f32[512,128]{1,0:T(8,128)S(1)}, f32[512,128]{1,0:T(8,128)}, u32[]{:S(2)}) copy-start(f32[512,128]{1,0:T(8,128)} %get-tuple-element.42) | copy-start | bytes 786436
  81.4 17.3 %copy-start.12 = (f32[256,128]{1,0:T(8,128)S(1)}, f32[256,128]{1,0:T(8,128)}, u32[]{:S(2)}) copy-start(f32[256,128]{1,0:T(8,128)} %get-tuple-element.43) | copy-start | bytes 393220
  81.5 24.0 %copy-start.5 = (f32[512,128]{1,0:T(8,128)S(1)}, f32[512,128]{1,0:T(8,128)}, u32[]{:S(2)}) copy-start(f32[512,128]{1,0:T(8,128)} %copy-done.4) | copy-start | bytes 786436
  81.5 24.0 %copy-start.7 = (f32[512,128]{1,0:T(8,128)S(1)}, f32[512,128]{1,0:T(8,128)}, u32[]{:S(2)}) copy-start(f32[512,128]{1,0:T(8,128)} %copy-done.6) | copy-start | bytes 786436
  91.6 9.6 %collective-permute-start.6 = (f32[512,128]{1,0:T(8,128)S(1)}, f32[512,128]{1,0:T(8,128)S(1)}, u32[]{:S(2)}, u32[]{:S(2)}) collective-permute-start(f32[512,128]{1,0:T(8,128)S(1)} %get-tuple-element.33), channel_id=1, source_target_pairs={{0,8},{8,0},{16,24},{24,16},{1,9},{9,1},{17,25},{25,17},{2,10},{10... | collective-permute-start | bytes 786440 | tf_op jit(solution)/shard_map/ppermute | solution.py:371
  91.6 9.6 %collective-permute-start.7 = (f32[512,128]{1,0:T(8,128)S(1)}, f32[512,128]{1,0:T(8,128)S(1)}, u32[]{:S(2)}, u32[]{:S(2)}) collective-permute-start(f32[512,128]{1,0:T(8,128)S(1)} %get-tuple-element.34), channel_id=1, source_target_pairs={{0,16},{8,24},{16,0},{24,8},{1,17},{9,25},{17,1},{25,9},{2,18},{10... | collective-permute-start | bytes 786440 | tf_op jit(solution)/shard_map/ppermute | solution.py:371
  93.1 12.4 %collective-permute-start.8 = (f32[512,128]{1,0:T(8,128)S(1)}, f32[512,128]{1,0:T(8,128)S(1)}, u32[]{:S(2)}, u32[]{:S(2)}) collective-permute-start(f32[512,128]{1,0:T(8,128)S(1)} %get-tuple-element.35), channel_id=1, source_target_pairs={{0,24},{8,16},{16,8},{24,0},{1,25},{9,17},{17,9},{25,1},{2,26},{10... | collective-permute-start | bytes 786440 | tf_op jit(solution)/shard_map/ppermute | solution.py:371
  93.5 20.8 %collective-permute-start.12 = (f32[512,128]{1,0:T(8,128)S(1)}, f32[512,128]{1,0:T(8,128)S(1)}, u32[]{:S(2)}, u32[]{:S(2)}) collective-permute-start(f32[512,128]{1,0:T(8,128)S(1)} %copy-done.11), channel_id=1, source_target_pairs={{0,4},{1,5},{2,6},{3,7},{4,0},{5,1},{6,2},{7,3},{8,12},{9,13},{10,... | collective-permute-start | bytes 786440 | tf_op jit(solution)/shard_map/ppermute | solution.py:371
  98.7 12.1 %collective-permute-start.13 = (f32[256,128]{1,0:T(8,128)S(1)}, f32[256,128]{1,0:T(8,128)S(1)}, u32[]{:S(2)}, u32[]{:S(2)}) collective-permute-start(f32[256,128]{1,0:T(8,128)S(1)} %copy-done.12), channel_id=1, source_target_pairs={{0,6},{1,7},{2,4},{3,5},{4,2},{5,3},{6,0},{7,1},{8,14},{9,15},{10,... | collective-permute-start | bytes 393224 | tf_op jit(solution)/shard_map/ppermute | solution.py:371
where the time goes:
time: 116 us; the launch traced here: 115 us
  waiting for transfers between devices  50.3 us (43%)
  starting transfers between devices  31.9 us (28%)
  Pallas kernels  30.2 us (26%)
  local copies, waits for them, and re-layouts  2.5 us (2%)
    ppermute x14, waiting for transfers between devices, exchange(): return lax.ppermute(block, axis, [(i, i ^ distance) for i in range(size)])  28.3 us
    all_to_all x2, waiting for transfers between devices, fast_path(): recv.append(lax.all_to_all(v_blocks, ('pen', 'grp'), 0, 0, tiled=True))  22.1 us
    ppermute x14, starting transfers between devices, exchange(): return lax.ppermute(block, axis, [(i, i ^ distance) for i in range(size)])  20.6 us
    all_to_all x2, starting transfers between devices, fast_path(): recv.append(lax.all_to_all(v_blocks, ('pen', 'grp'), 0, 0, tiled=True))  11.3 us
    pallas_call x1, Pallas kernels, fast_path(): kernel_call(functools.partial(first_kernel, sizes, half_pens), [jax.Shape...  8.3 us
    pallas_call x2, Pallas kernels, fast_path(): kernel_call(functools.partial(second_kernel, sizes, tile), jax.ShapeDtype...  8.22 us
    pallas_call x2, Pallas kernels, fast_path(): kernel_call(circulant_kernel, [jax.ShapeDtypeStruct((group_rows, lanes),...  7.5 us
    pallas_call x1, Pallas kernels, fast_path(): kernel_call(functools.partial(final_kernel, sizes, early, late), [jax.Sha...  2.93 us
  transfers between devices with their start and end apart: 16, of which 8 were waited for; matrix products, arithmetic and copies ran while one was open for 0% of the time, Pallas kernels for 22%

commit v1 on v0

--- a/solution.py
+++ b/solution.py
@@ -10,8 +10,9 @@
 from jax.sharding import PartitionSpec as P
 
 
-LAST = ((4, 0), (6, 1))
+LAST = ((4, 0),)
 PARTS = {6: 2}
+SLOTS = (0,)
 f32 = jnp.float32
 bf16 = jnp.bfloat16
 
@@ -160,12 +161,21 @@
         copy.wait()
 
 
-def first_kernel(sizes, slots, order_ref, swap_ref, field_hbm, *refs):
+def first_kernel(sizes, slots, order_hbm, swap_hbm, field_hbm, *refs):
     planes, rows, slab, pens = sizes
-    outs, (field_ref, table_ref, waves_ref, piece_ref, sems) = refs[:-5], refs[-5:]
-    pieces = cut_pieces(range(pens))
-    load = pltpu.make_async_copy(field_hbm, field_ref, sems.at[len(outs)])
-    load.start()
+    outs = refs[:-8]
+    order_ref, swap_ref, field_ref, table_ref, waves_ref, piece_ref, load_sems, sems = refs[-8:]
+    distances = [k for slot in slots for k in (slot, pens - 1 - slot)]
+    pieces = cut_pieces(distances)
+    loads = [
+        pltpu.make_async_copy(*pair, load_sems.at[i])
+        for i, pair in enumerate(
+            ((order_hbm, order_ref), (field_hbm, field_ref), (swap_hbm, swap_ref))
+        )
+    ]
+    for load in loads:
+        load.start()
+    loads[0].wait()
     length = order_ref.shape[1]
     pen = lax.axis_index("pen")
     upper = pen >= pens // 2
@@ -175,8 +185,9 @@
         first = pl.multiple_of(block * slab, slab)
         waves_ref[:, i * slab : (i + 1) * slab] = order_ref[:, pl.ds(first, slab)]
     fill_table(waves_ref[...], table_ref, length)
-    load.wait()
+    loads[1].wait()
     fields = load_quarters(field_ref)
+    loads[2].wait()
     lanes = 128
     step = 2 * planes * (slab // lanes)
     copies = []
@@ -196,7 +207,7 @@
                         piece_ref[to, pl.ds(at, rows, stride=step), :] = piece[
                             plane * rows : (plane + 1) * rows, tile * lanes : (tile + 1) * lanes
                         ]
-        for to, slot in ((2 * i, slots[i]), (2 * i + 1, pens - 1 - slots[i])):
+        for to, slot in list(enumerate(distances))[2 * i : 2 * i + 2]:
             for n, (other, part, parts) in enumerate(pieces):
                 if other != slot:
                     continue
@@ -376,7 +387,6 @@
     length_y = v.shape[1]
     group_rows = rows * pens
     length_z = group_rows * groups
-    half = length_y // 2
     lanes = 128
     pen = lax.axis_index("pen")
     order = ky_order[None, :]
@@ -406,23 +416,29 @@
     swap = jnp.asarray(np.eye(slab)[::-1].copy(), bf16)
     size = rows * 2 * planes * slab // lanes
     pieces = cut_pieces(range(pens))
-    half_pens = list(range(pens // 2))
-    firsts = kernel_call(
-        functools.partial(first_kernel, sizes, half_pens),
-        [jax.ShapeDtypeStruct((size // parts, lanes), f32) for _, _, parts in pieces],
-        "vvh>" + "h" * len(pieces),
-        flops,
-        2**21,
-        60,
-        [
-            field,
-            pltpu.VMEM((2, length_y // 4, length_y), bf16),
-            pltpu.VMEM((1, half), jnp.int32),
-            pltpu.VMEM((pens, size, lanes), f32),
-            dma((len(pieces) + 1,)),
-        ],
-    )(order, swap, u)
-    firsts = dict(zip(pieces, firsts))
+    firsts = {}
+    for slots in (SLOTS, [k for k in range(pens // 2) if k not in SLOTS]):
+        wide = len(slots) * slab
+        ours = cut_pieces([k for slot in slots for k in (slot, pens - 1 - slot)])
+        values = kernel_call(
+            functools.partial(first_kernel, sizes, slots),
+            [jax.ShapeDtypeStruct((size // parts, lanes), f32) for _, _, parts in ours],
+            "hhh>" + "h" * len(ours),
+            flops // pens * len(slots),
+            2**21,
+            60,
+            [
+                pltpu.VMEM((1, length_y), jnp.int32),
+                pltpu.VMEM((slab, slab), bf16),
+                field,
+                pltpu.VMEM((2, length_y // 4, 2 * wide), bf16),
+                pltpu.VMEM((1, wide), jnp.int32),
+                pltpu.VMEM((2 * len(slots), size, lanes), f32),
+                dma((3,)),
+                dma((len(ours),)),
+            ],
+        )(order, swap, u)
+        firsts.update(zip(ours, values))
     circulant = kernel_call(
         table_kernel,
         jax.ShapeDtypeStruct((2, 11, length_z // 8, length_z // 8), bf16),
@@ -430,7 +446,7 @@
         2**24,
         2**21,
         16,
-    )(firsts[pieces[0]])
+    )(firsts[pieces[-2]])
     arrived = {}
     for piece in pieces:
         k, _, _ = piece

time: 116 us -> 119 us (1.026)
  waiting for transfers between devices: 50.3 us -> 46 us
  starting transfers between devices: 31.9 us -> 35.3 us
  local copies, waits for them, and re-layouts: 2.5 us -> 4.49 us
  Pallas kernels: 30.2 us -> 31.7 us
    ppermute x14, waiting for transfers between devices: 28.3 us -> 23.9 us  [exchange(): return lax.ppermute(block, axis, [(i, i ^ distance) for i in range(size)])]
    ppermute x14, starting transfers between devices: 20.6 us -> 24.1 us  [exchange(): return lax.ppermute(block, axis, [(i, i ^ distance) for i in range(size)])]
    unnamed x26 -> x28, local copies, waits for them, and re-layouts: 2.5 us -> 4.49 us
    pallas_call x1 -> x2, Pallas kernels: 8.3 us -> 10.1 us  [fast_path(): kernel_call(functools.partial(first_kernel, sizes, slots), [jax.ShapeDtyp...]
  transfers between devices with their start and end apart: 16 -> 16, of which waited for: 8 -> 6; matrix products, arithmetic and copies ran while one was open for 0% -> 0% of each run, Pallas kernels for 22% -> 23%
where the time goes in v1:
time: 119 us; the launch traced here: 118 us
  waiting for transfers between devices  46 us (39%)
  starting transfers between devices  35.3 us (30%)
  Pallas kernels  31.7 us (27%)
  local copies, waits for them, and re-layouts  4.49 us (4%)
    ppermute x14, starting transfers between devices, exchange(): return lax.ppermute(block, axis, [(i, i ^ distance) for i in range(size)])  24.1 us
    ppermute x14, waiting for transfers between devices, exchange(): return lax.ppermute(block, axis, [(i, i ^ distance) for i in range(size)])  23.9 us
    all_to_all x2, waiting for transfers between devices, fast_path(): recv.append(lax.all_to_all(v_blocks, ('pen', 'grp'), 0, 0, tiled=True))  22.1 us
    all_to_all x2, starting transfers between devices, fast_path(): recv.append(lax.all_to_all(v_blocks, ('pen', 'grp'), 0, 0, tiled=True))  11.3 us
    pallas_call x2, Pallas kernels, fast_path(): kernel_call(functools.partial(first_kernel, sizes, slots), [jax.ShapeDtyp...  10.1 us
    pallas_call x2, Pallas kernels, fast_path(): kernel_call(functools.partial(second_kernel, sizes, tile), jax.ShapeDtype...  8.22 us
    pallas_call x2, Pallas kernels, fast_path(): kernel_call(circulant_kernel, [jax.ShapeDtypeStruct((group_rows, lanes),...  7.24 us
    unnamed x28, local copies, waits for them, and re-layouts  4.49 us
  transfers between devices with their start and end apart: 16, of which 6 were waited for; matrix products, arithmetic and copies ran while one was open for 0% of the time, Pallas kernels for 23%

profile of v1, /device:TPU:0, one launch (start us, length us, event | category | flops | bytes accessed | tf_op | source)
XLA Modules:
  0.0 117.9 jit_solution(2434388021493921097)
XLA Ops:
  0.0 4.1 %shard_map.69 = f32[8,4,64,128]{3,2,1,0:T(8,128)} custom-call(s32[1,2048]{1,0:T(1,128)} %bitcast.10, f32[128,2048]{1,0:T(8,128)} %bitcast.17), custom_call_target="tpu_custom_call" | custom-call | flops 1610612736 | bytes 2097152 | tf_op jit(solution)/shard_map/pallas_call | solution.py:399
  4.1 7.3 %all-to-all-start.1 = ((f32[32,64,128]{2,1,0:T(8,128)}), f32[32,64,128]{2,1,0:T(8,128)S(1)}, u32[]{:S(2)}, u32[]{:S(2)}) async-start(f32[32,64,128]{2,1,0:T(8,128)} %bitcast.16), calls=%async_computation.1 | async-start | bytes 2097152 | tf_op jit(solution)/shard_map/all_to_all | solution.py:415
  11.5 4.1 %shard_map.66 = f32[8,4,64,128]{3,2,1,0:T(8,128)} custom-call(s32[1,2048]{1,0:T(1,128)} %bitcast.11, f32[128,2048]{1,0:T(8,128)} %bitcast.18), custom_call_target="tpu_custom_call" | custom-call | flops 1610612736 | bytes 2097152 | tf_op jit(solution)/shard_map/pallas_call | solution.py:399
  15.6 22.1 %all-to-all-done.1.recv_ref = f32[32,64,128]{2,1,0:T(8,128)S(1)} async-done(((f32[32,64,128]{2,1,0:T(8,128)}), f32[32,64,128]{2,1,0:T(8,128)S(1)}, u32[]{:S(2)}, u32[]{:S(2)}) %all-to-all-start.1) | async-done | bytes 1048608 | tf_op jit(solution)/shard_map/all_to_all | solution.py:415
  37.7 0.0 copy-start
  37.7 3.9 %all-to-all-start = ((f32[32,64,128]{2,1,0:T(8,128)}), f32[32,64,128]{2,1,0:T(8,128)}, u32[]{:S(2)}, u32[]{:S(2)}) async-start(f32[32,64,128]{2,1,0:T(8,128)} %bitcast.15), calls=%async_computation | async-start | bytes 2097152 | tf_op jit(solution)/shard_map/all_to_all | solution.py:415
  41.6 0.0 copy-start.11
  41.6 0.0 copy-start.12
  41.6 6.6 %shard_map.65 = (f32[512,128]{1,0:T(8,128)}, f32[256,128]{1,0:T(8,128)}, f32[256,128]{1,0:T(8,128)}, f32[512,128]{1,0:T(8,128)}, f32[512,128]{1,0:T(8,128)}, /*index=5*/f32[512,128]{1,0:T(8,128)}, f32[512,128]{1,0:T(8,128)}) custom-call(s32[1,2048]{1,0:T(1,128)} %bitcast.12, bf16[256,256]{1,0:T(8,128)(2,1)} %constant.12.clone.swap_hbm, f32[128,2048]{1,0:T(8,128)} %bitcast.19), custom_call_target="tpu_custom_call" | custom-call | flops 1207959552 | bytes 2097152 | tf_op jit(solution)/shard_map/pallas_call | solution.py:423
  48.2 0.0 copy-done
  48.2 3.6 %collective-permute-start.5 = (f32[256,128]{1,0:T(8,128)}, f32[256,128]{1,0:T(8,128)S(1)}, u32[]{:S(2)}, u32[]{:S(2)}) collective-permute-start(f32[256,128]{1,0:T(8,128)} %get-tuple-element.30.after_ref), channel_id=1, source_target_pairs={{0,6},{1,7},{2,4},{3,5},{4,2},{5,3},{6,0},{7,1},{8,14},{9,15},{10,... | collective-permute-start | bytes 393224 | tf_op jit(solution)/shard_map/ppermute | solution.py:382
  51.8 1.5 %collective-permute-start = (f32[512,128]{1,0:T(8,128)}, f32[512,128]{1,0:T(8,128)S(1)}, u32[]{:S(2)}, u32[]{:S(2)}) collective-permute-start(f32[512,128]{1,0:T(8,128)} %get-tuple-element.25), channel_id=1, source_target_pairs={{0,1},{1,0},{2,3},{3,2},{4,5},{5,4},{6,7},{7,6},{8,9},{9,8},{10,11... | collective-permute-start | bytes 786440 | tf_op jit(solution)/shard_map/ppermute | solution.py:382
  53.3 0.0 collective-permute-start.1
  53.3 2.0 %collective-permute-start.2 = (f32[512,128]{1,0:T(8,128)}, f32[512,128]{1,0:T(8,128)}, u32[]{:S(2)}, u32[]{:S(2)}) collective-permute-start(f32[512,128]{1,0:T(8,128)} %get-tuple-element.27), channel_id=1, source_target_pairs={{0,3},{1,2},{2,1},{3,0},{4,7},{5,6},{6,5},{7,4},{8,11},{9,10},{10,... | collective-permute-start | bytes 786440 | tf_op jit(solution)/shard_map/ppermute | solution.py:382
  55.3 0.3 collective-permute-start.4
  55.6 0.0 copy-done.11
  55.6 0.0 copy-done.12
  55.6 0.0 copy-start.5
  55.6 0.9 copy-done.5
  56.5 0.0 copy-start.6
  56.5 2.5 %shard_map.67.table_ref = bf16[2,11,256,256]{3,2,1,0:T(8,128)(2,1)S(1)} custom-call(f32[256,128]{1,0:T(8,128)S(1)} %copy-done.5), custom_call_target="tpu_custom_call" | custom-call | flops 16777216 | bytes 2097152 | tf_op jit(solution)/shard_map/pallas_call | solution.py:442
  59.0 3.6 %shard_map.64 = (f32[512,128]{1,0:T(8,128)}, f32[512,128]{1,0:T(8,128)}) custom-call(s32[1,2048]{1,0:T(1,128)} %bitcast.13, bf16[256,256]{1,0:T(8,128)(2,1)} %constant.12.clone.swap_hbm, f32[128,2048]{1,0:T(8,128)} %bitcast.20), custom_call_target="tpu_custom_call" | custom-call | flops 402653184 | bytes 2097152 | tf_op jit(solution)/shard_map/pallas_call | solution.py:423
  62.6 0.0 copy-done.6
  62.6 0.0 copy-start.1
  62.6 1.2 %copy-done.1 = f32[32,64,128]{2,1,0:T(8,128)S(1)} copy-done((f32[32,64,128]{2,1,0:T(8,128)S(1)}, f32[32,64,128]{2,1,0:T(8,128)}, u32[]{:S(2)}) %copy-start.1) | copy-done | bytes 1048600
  63.8 3.3 %shard_map.70 = (f32[512,128]{1,0:T(8,128)S(1)}, f32[512,128]{1,0:T(8,128)}, f32[512,128]{1,0:T(8,128)}, f32[512,128]{1,0:T(8,128)S(1)}) custom-call(f32[32,64,128]{2,1,0:T(8,128)S(1)} %copy-done.1, bf16[2,11,256,256]{3,2,1,0:T(8,128)(2,1)S(1)} %shard_map.67.table_ref, bf16[256,256]{1,0:T(8,128)(2,1)S(1)} %broadcast_select_fusion.turn_ref), custom_call_target="tpu_custom_call" | custom-call | flops 1610612736 | bytes 4194304 | tf_op jit(solution)/shard_map/pallas_call | solution.py:458
  67.1 0.0 copy-start.3
  67.1 0.7 copy-done.3
  67.8 0.0 copy-start.9
  67.8 0.7 copy-done.9
  68.5 0.0 collective-permute-done.5.refs_6_
  68.6 6.1 %collective-permute-start.3 = (f32[512,128]{1,0:T(8,128)}, f32[512,128]{1,0:T(8,128)}, u32[]{:S(2)}, u32[]{:S(2)}) collective-permute-start(f32[512,128]{1,0:T(8,128)} %get-tuple-element.28), channel_id=1, source_target_pairs={{0,5},{1,4},{2,7},{3,6},{4,1},{5,0},{6,3},{7,2},{8,13},{9,12},{10,... | collective-permute-start | bytes 786440 | tf_op jit(solution)/shard_map/ppermute | solution.py:382
  74.6 5.8 %collective-permute-done.4.refs_5_ = f32[256,128]{1,0:T(8,128)} collective-permute-done((f32[256,128]{1,0:T(8,128)}, f32[256,128]{1,0:T(8,128)}, u32[]{:S(2)}, u32[]{:S(2)}) %collective-permute-start.4) | collective-permute-done | bytes 131104 | tf_op jit(solution)/shard_map/ppermute | solution.py:382
  80.5 1.6 %collective-permute-start.6 = (f32[512,128]{1,0:T(8,128)}, f32[512,128]{1,0:T(8,128)}, u32[]{:S(2)}, u32[]{:S(2)}) collective-permute-start(f32[512,128]{1,0:T(8,128)} %get-tuple-element.31), channel_id=1, source_target_pairs={{0,7},{1,6},{2,5},{3,4},{4,3},{5,2},{6,1},{7,0},{8,15},{9,14},{10,... | collective-permute-start | bytes 786440 | tf_op jit(solution)/shard_map/ppermute | solution.py:382
  82.0 0.0 collective-permute-done.refs_1_
  82.0 0.0 collective-permute-start.10
  82.0 0.0 collective-permute-done.1.refs_2_
  82.0 1.5 %collective-permute-start.11 = (f32[512,128]{1,0:T(8,128)}, f32[512,128]{1,0:T(8,128)}, u32[]{:S(2)}, u32[]{:S(2)}) collective-permute-start(f32[512,128]{1,0:T(8,128)} %get-tuple-element.38), channel_id=1, source_target_pairs={{0,16},{8,24},{16,0},{24,8},{1,17},{9,25},{17,1},{25,9},{2,18},{10... | collective-permute-start | bytes 786440 | tf_op jit(solution)/shard_map/ppermute | solution.py:382
  83.5 0.0 all-to-all-done.recv_ref
  83.5 0.9 copy-done.7
  84.4 0.0 copy-start.8
  84.4 3.9 %shard_map.68 = (f32[512,128]{1,0:T(8,128)S(1)}, f32[512,128]{1,0:T(8,128)S(1)}, f32[512,128]{1,0:T(8,128)S(1)}, f32[512,128]{1,0:T(8,128)S(1)}) custom-call(f32[32,64,128]{2,1,0:T(8,128)} %all-to-all-done.recv_ref, bf16[2,11,256,256]{3,2,1,0:T(8,128)(2,1)S(1)} %shard_map.67.table_ref, bf16[256,256]{1,0:T(8,128)(2,1)S(1)} %copy-done.7), custom_call_target="tpu_custom_call" | custom-call | flops 1610612736 | bytes 4194304 | tf_op jit(solution)/shard_map/pallas_call | solution.py:458
  88.4 0.0 collective-permute-done.2.refs_3_
  88.4 0.0 copy-done.10
  88.4 0.5 collective-permute-start.12
  88.9 8.3 %collective-permute-done.3.refs_4_ = f32[512,128]{1,0:T(8,128)} collective-permute-done((f32[512,128]{1,0:T(8,128)}, f32[512,128]{1,0:T(8,128)}, u32[]{:S(2)}, u32[]{:S(2)}) %collective-permute-start.3) | collective-permute-done | bytes 262176 | tf_op jit(solution)/shard_map/ppermute | solution.py:382
  97.2 0.0 collective-permute-start.7
  97.2 0.0 collective-permute-done.6.refs_7_
  97.2 1.5 %collective-permute-start.8 = (f32[512,128]{1,0:T(8,128)S(1)}, f32[512,128]{1,0:T(8,128)S(1)}, u32[]{:S(2)}, u32[]{:S(2)}) collective-permute-start(f32[512,128]{1,0:T(8,128)S(1)} %get-tuple-element.34), channel_id=1, source_target_pairs={{0,16},{8,24},{16,0},{24,8},{1,17},{9,25},{17,1},{25,9},{2,18},{10... | collective-permute-start | bytes 786440 | tf_op jit(solution)/shard_map/ppermute | solution.py:382
  98.7 0.0 collective-permute-done.10.refs_13_
  98.7 0.4 collective-permute-start.9
  99.0 0.0 collective-permute-done.11.refs_14_
  99.1 0.0 copy-done.13
  99.1 5.3 %collective-permute-start.13 = (f32[512,128]{1,0:T(8,128)S(1)}, f32[512,128]{1,0:T(8,128)S(1)}, u32[]{:S(2)}, u32[]{:S(2)}) collective-permute-start(f32[512,128]{1,0:T(8,128)S(1)} %copy-done.13), channel_id=1, source_target_pairs={{0,4},{1,5},{2,6},{3,7},{4,0},{5,1},{6,2},{7,3},{8,12},{9,13},{10,... | collective-permute-start | bytes 786440 | tf_op jit(solution)/shard_map/ppermute | solution.py:382
  104.3 0.0 collective-permute-done.12.refs_15_
  104.3 0.0 collective-permute-done.7.refs_9_
  104.3 2.0 %collective-permute-done.8.refs_10_ = f32[512,128]{1,0:T(8,128)S(1)} collective-permute-done((f32[512,128]{1,0:T(8,128)S(1)}, f32[512,128]{1,0:T(8,128)S(1)}, u32[]{:S(2)}, u32[]{:S(2)}) %collective-permute-start.8) | collective-permute-done | bytes 262176 | tf_op jit(solution)/shard_map/ppermute | solution.py:382
  106.4 4.7 %collective-permute-done.9.refs_11_ = f32[512,128]{1,0:T(8,128)S(1)} collective-permute-done((f32[512,128]{1,0:T(8,128)S(1)}, f32[512,128]{1,0:T(8,128)S(1)}, u32[]{:S(2)}, u32[]{:S(2)}) %collective-permute-start.9) | collective-permute-done | bytes 262176 | tf_op jit(solution)/shard_map/ppermute | solution.py:382
  111.1 0.0 copy-done.2
  111.1 0.0 copy-done.4
  111.1 0.0 copy-done.8
  111.1 2.9 %shard_map.71 = (f32[4096,128]{1,0:T(8,128)}, f32[512,128]{1,0:T(8,128)S(1)}) custom-call(s32[1,2048]{1,0:T(1,128)S(1)} %bitcast.14, f32[512,128]{1,0:T(8,128)S(1)} %copy-done.2, f32[512,128]{1,0:T(8,128)S(1)} %collective-permute-done.refs_1_, f32[512,128]{1,0:T(8,128)S(1)} %collective-permute-done.1.refs_2_, f32[512,128]{1,0:T(8,128)} %collective-permute-done.2.refs_3_, ...), custom_call_target="tpu_custom_call" | custom-call | flops 1048576 | bytes 1048576 | tf_op jit(solution)/shard_map/pallas_call | solution.py:472
  114.0 3.0 %collective-permute-done.13.refs_1_ = f32[512,128]{1,0:T(8,128)S(1)} collective-permute-done((f32[512,128]{1,0:T(8,128)S(1)}, f32[512,128]{1,0:T(8,128)S(1)}, u32[]{:S(2)}, u32[]{:S(2)}) %collective-permute-start.13) | collective-permute-done | bytes 262176 | tf_op jit(solution)/shard_map/ppermute | solution.py:382
  117.0 0.7 shard_map.72
  (6 shorter events, 0.0 us)
Async XLA Ops:
  4.1 33.5 %all-to-all-start.1 = ((f32[32,64,128]{2,1,0:T(8,128)}), f32[32,64,128]{2,1,0:T(8,128)S(1)}, u32[]{:S(2)}, u32[]{:S(2)}) async-start(f32[32,64,128]{2,1,0:T(8,128)} %bitcast.16), calls=%async_computation.1 | async-start | bytes 2097152 | tf_op jit(solution)/shard_map/all_to_all | solution.py:415
  37.7 10.5 %copy-start = (f32[32,64,128]{2,1,0:T(8,128)}, f32[32,64,128]{2,1,0:T(8,128)S(1)}, u32[]{:S(2)}) copy-start(f32[32,64,128]{2,1,0:T(8,128)S(1)} %all-to-all-done.1.recv_ref) | copy-start | bytes 3145732
  37.7 45.8 %all-to-all-start = ((f32[32,64,128]{2,1,0:T(8,128)}), f32[32,64,128]{2,1,0:T(8,128)}, u32[]{:S(2)}, u32[]{:S(2)}) async-start(f32[32,64,128]{2,1,0:T(8,128)} %bitcast.15), calls=%async_computation | async-start | bytes 2097152 | tf_op jit(solution)/shard_map/all_to_all | solution.py:415
  41.6 14.0 %copy-start.11 = (bf16[256,256]{1,0:T(8,128)(2,1)S(1)}, bf16[256,256]{1,0:T(8,128)(2,1)}, u32[]{:S(2)}) copy-start(bf16[256,256]{1,0:T(8,128)(2,1)} %constant.13.clone) | copy-start | bytes 393220
  41.6 14.0 %copy-start.12 = (bf16[256,256]{1,0:T(8,128)(2,1)S(1)}, bf16[256,256]{1,0:T(8,128)(2,1)}, u32[]{:S(2)}) copy-start(bf16[256,256]{1,0:T(8,128)(2,1)} %constant.14.clone) | copy-start | bytes 393220
  48.2 20.3 %collective-permute-start.5 = (f32[256,128]{1,0:T(8,128)}, f32[256,128]{1,0:T(8,128)S(1)}, u32[]{:S(2)}, u32[]{:S(2)}) collective-permute-start(f32[256,128]{1,0:T(8,128)} %get-tuple-element.30.after_ref), channel_id=1, source_target_pairs={{0,6},{1,7},{2,4},{3,5},{4,2},{5,3},{6,0},{7,1},{8,14},{9,15},{10,... | collective-permute-start | bytes 393224 | tf_op jit(solution)/shard_map/ppermute | solution.py:382
  51.8 30.2 %collective-permute-start = (f32[512,128]{1,0:T(8,128)}, f32[512,128]{1,0:T(8,128)S(1)}, u32[]{:S(2)}, u32[]{:S(2)}) collective-permute-start(f32[512,128]{1,0:T(8,128)} %get-tuple-element.25), channel_id=1, source_target_pairs={{0,1},{1,0},{2,3},{3,2},{4,5},{5,4},{6,7},{7,6},{8,9},{9,8},{10,11... | collective-permute-start | bytes 786440 | tf_op jit(solution)/shard_map/ppermute | solution.py:382
  53.3 28.7 %collective-permute-start.1 = (f32[512,128]{1,0:T(8,128)}, f32[512,128]{1,0:T(8,128)S(1)}, u32[]{:S(2)}, u32[]{:S(2)}) collective-permute-start(f32[512,128]{1,0:T(8,128)} %get-tuple-element.26), channel_id=1, source_target_pairs={{0,2},{1,3},{2,0},{3,1},{4,6},{5,7},{6,4},{7,5},{8,10},{9,11},{10,... | collective-permute-start | bytes 786440 | tf_op jit(solution)/shard_map/ppermute | solution.py:382
  53.3 35.0 %collective-permute-start.2 = (f32[512,128]{1,0:T(8,128)}, f32[512,128]{1,0:T(8,128)}, u32[]{:S(2)}, u32[]{:S(2)}) collective-permute-start(f32[512,128]{1,0:T(8,128)} %get-tuple-element.27), channel_id=1, source_target_pairs={{0,3},{1,2},{2,1},{3,0},{4,7},{5,6},{6,5},{7,4},{8,11},{9,10},{10,... | collective-permute-start | bytes 786440 | tf_op jit(solution)/shard_map/ppermute | solution.py:382
  55.3 25.1 %collective-permute-start.4 = (f32[256,128]{1,0:T(8,128)}, f32[256,128]{1,0:T(8,128)}, u32[]{:S(2)}, u32[]{:S(2)}) collective-permute-start(f32[256,128]{1,0:T(8,128)} %get-tuple-element.29), channel_id=1, source_target_pairs={{0,6},{1,7},{2,4},{3,5},{4,2},{5,3},{6,0},{7,1},{8,14},{9,15},{10,... | collective-permute-start | bytes 393224 | tf_op jit(solution)/shard_map/ppermute | solution.py:382
  55.6 0.9 copy-start.5
  56.5 6.0 %copy-start.6 = (bf16[256,256]{1,0:T(8,128)(2,1)}, bf16[256,256]{1,0:T(8,128)(2,1)S(1)}, u32[]{:S(2)}) copy-start(bf16[256,256]{1,0:T(8,128)(2,1)S(1)} %broadcast_select_fusion.turn_ref) | copy-start | bytes 393220
  62.6 1.2 %copy-start.1 = (f32[32,64,128]{2,1,0:T(8,128)S(1)}, f32[32,64,128]{2,1,0:T(8,128)}, u32[]{:S(2)}) copy-start(f32[32,64,128]{2,1,0:T(8,128)} %copy-done) | copy-start | bytes 3145732
  67.1 0.7 copy-start.3
  67.8 0.7 copy-start.9
  68.6 28.6 %collective-permute-start.3 = (f32[512,128]{1,0:T(8,128)}, f32[512,128]{1,0:T(8,128)}, u32[]{:S(2)}, u32[]{:S(2)}) collective-permute-start(f32[512,128]{1,0:T(8,128)} %get-tuple-element.28), channel_id=1, source_target_pairs={{0,5},{1,4},{2,7},{3,6},{4,1},{5,0},{6,3},{7,2},{8,13},{9,12},{10,... | collective-permute-start | bytes 786440 | tf_op jit(solution)/shard_map/ppermute | solution.py:382
  80.5 16.7 %collective-permute-start.6 = (f32[512,128]{1,0:T(8,128)}, f32[512,128]{1,0:T(8,128)}, u32[]{:S(2)}, u32[]{:S(2)}) collective-permute-start(f32[512,128]{1,0:T(8,128)} %get-tuple-element.31), channel_id=1, source_target_pairs={{0,7},{1,6},{2,5},{3,4},{4,3},{5,2},{6,1},{7,0},{8,15},{9,14},{10,... | collective-permute-start | bytes 786440 | tf_op jit(solution)/shard_map/ppermute | solution.py:382
  82.0 16.6 %collective-permute-start.10 = (f32[512,128]{1,0:T(8,128)}, f32[512,128]{1,0:T(8,128)}, u32[]{:S(2)}, u32[]{:S(2)}) collective-permute-start(f32[512,128]{1,0:T(8,128)} %get-tuple-element.37), channel_id=1, source_target_pairs={{0,8},{8,0},{16,24},{24,16},{1,9},{9,1},{17,25},{25,17},{2,10},{10... | collective-permute-start | bytes 786440 | tf_op jit(solution)/shard_map/ppermute | solution.py:382
  82.0 17.0 %collective-permute-start.11 = (f32[512,128]{1,0:T(8,128)}, f32[512,128]{1,0:T(8,128)}, u32[]{:S(2)}, u32[]{:S(2)}) collective-permute-start(f32[512,128]{1,0:T(8,128)} %get-tuple-element.38), channel_id=1, source_target_pairs={{0,16},{8,24},{16,0},{24,8},{1,17},{9,25},{17,1},{25,9},{2,18},{10... | collective-permute-start | bytes 786440 | tf_op jit(solution)/shard_map/ppermute | solution.py:382
  83.5 0.9 copy-start.7
  84.4 4.0 %copy-start.10 = (f32[512,128]{1,0:T(8,128)S(1)}, f32[512,128]{1,0:T(8,128)}, u32[]{:S(2)}) copy-start(f32[512,128]{1,0:T(8,128)} %copy-done.9) | copy-start | bytes 786436
  84.4 14.6 %copy-start.13 = (f32[512,128]{1,0:T(8,128)S(1)}, f32[512,128]{1,0:T(8,128)}, u32[]{:S(2)}) copy-start(f32[512,128]{1,0:T(8,128)} %get-tuple-element.41) | copy-start | bytes 786436
  84.4 26.7 %copy-start.2 = (f32[512,128]{1,0:T(8,128)S(1)}, f32[512,128]{1,0:T(8,128)}, u32[]{:S(2)}) copy-start(f32[512,128]{1,0:T(8,128)} %get-tuple-element.24.refs_0_) | copy-start | bytes 786436
  84.4 26.7 %copy-start.4 = (f32[512,128]{1,0:T(8,128)S(1)}, f32[512,128]{1,0:T(8,128)}, u32[]{:S(2)}) copy-start(f32[512,128]{1,0:T(8,128)} %copy-done.3) | copy-start | bytes 786436
  84.4 26.6 %copy-start.8 = (s32[2048]{0:T(1024)S(1)}, s32[2048]{0:T(1024)}, u32[]{:S(2)}) copy-start(s32[2048]{0:T(1024)} %param.8) | copy-start | bytes 24580
  88.4 15.9 %collective-permute-start.12 = (f32[512,128]{1,0:T(8,128)S(1)}, f32[512,128]{1,0:T(8,128)S(1)}, u32[]{:S(2)}, u32[]{:S(2)}) collective-permute-start(f32[512,128]{1,0:T(8,128)S(1)} %copy-done.10), channel_id=1, source_target_pairs={{0,24},{8,16},{16,8},{24,0},{1,25},{9,17},{17,9},{25,1},{2,26},{10... | collective-permute-start | bytes 786440 | tf_op jit(solution)/shard_map/ppermute | solution.py:382
  97.2 7.1 %collective-permute-start.7 = (f32[512,128]{1,0:T(8,128)S(1)}, f32[512,128]{1,0:T(8,128)S(1)}, u32[]{:S(2)}, u32[]{:S(2)}) collective-permute-start(f32[512,128]{1,0:T(8,128)S(1)} %get-tuple-element.33), channel_id=1, source_target_pairs={{0,8},{8,0},{16,24},{24,16},{1,9},{9,1},{17,25},{25,17},{2,10},{10... | collective-permute-start | bytes 786440 | tf_op jit(solution)/shard_map/ppermute | solution.py:382
  97.2 9.2 %collective-permute-start.8 = (f32[512,128]{1,0:T(8,128)S(1)}, f32[512,128]{1,0:T(8,128)S(1)}, u32[]{:S(2)}, u32[]{:S(2)}) collective-permute-start(f32[512,128]{1,0:T(8,128)S(1)} %get-tuple-element.34), channel_id=1, source_target_pairs={{0,16},{8,24},{16,0},{24,8},{1,17},{9,25},{17,1},{25,9},{2,18},{10... | collective-permute-start | bytes 786440 | tf_op jit(solution)/shard_map/ppermute | solution.py:382
  98.7 12.4 %collective-permute-start.9 = (f32[512,128]{1,0:T(8,128)S(1)}, f32[512,128]{1,0:T(8,128)S(1)}, u32[]{:S(2)}, u32[]{:S(2)}) collective-permute-start(f32[512,128]{1,0:T(8,128)S(1)} %get-tuple-element.35), channel_id=1, source_target_pairs={{0,24},{8,16},{16,8},{24,0},{1,25},{9,17},{17,9},{25,1},{2,26},{10... | collective-permute-start | bytes 786440 | tf_op jit(solution)/shard_map/ppermute | solution.py:382
  99.1 18.0 %collective-permute-start.13 = (f32[512,128]{1,0:T(8,128)S(1)}, f32[512,128]{1,0:T(8,128)S(1)}, u32[]{:S(2)}, u32[]{:S(2)}) collective-permute-start(f32[512,128]{1,0:T(8,128)S(1)} %copy-done.13), channel_id=1, source_target_pairs={{0,4},{1,5},{2,6},{3,7},{4,0},{5,1},{6,2},{7,3},{8,12},{9,13},{10,... | collective-permute-start | bytes 786440 | tf_op jit(solution)/shard_map/ppermute | solution.py:382
